TPU v7x, 512 devices: a whole 4x4x16 slice. The times are simulated.
512 devices in a mesh: dp: 32 (over y, z_lo), tensor: 16 (over x, z_hi, core).
Axes of the slice: x: 4, y: 4, z: 16 (z_hi: 2, z_lo: 8; z = z_hi * 8 + z_lo), core: 2. Of those that a mesh axis runs over, the one named last changes fastest.
Arguments:
- tokens: bfloat16 [16384, 4096], P(('dp', 'tensor')), may hold values from -6 to 6
- weight: bfloat16 [4096, 4096], P('tensor', 'dp'), may hold values from -0.09375 to 0.09375
Outputs:
- projected: bfloat16 [16384, 4096], P('dp', 'tensor')
All inputs are finite; a program needn't handle non-finite values.
Results may differ from a plain program's by a relative error of at most 0.0057.
Values may be sent and summed in bfloat16 or wider, within the bound.
A program may use at most 64 MiB of HBM per device.

v0:
```python
import jax
import jax.numpy as jnp
from jax import lax
from jax.sharding import PartitionSpec as P


def contract_last(left, right):
    return lax.dot_general(
        left, right, (((1,), (1,)), ((), ())), preferred_element_type=jnp.float32
    )


def contract_first(left, right):
    return lax.dot_general(
        left, right, (((0,), (0,)), ((), ())), preferred_element_type=jnp.float32
    )


def on_device(tokens, weight):
    col_slab = lax.all_gather(weight, "tensor", axis=0, tiled=True)
    term = contract_last(col_slab, weight)
    gram_cols = lax.psum(term, "dp").astype(jnp.bfloat16)
    update = 1.5 * weight.astype(jnp.float32) - 0.5 * contract_first(gram_cols, col_slab)
    ortho = update.astype(jnp.bfloat16)
    full_rows = lax.all_gather(ortho, "dp", axis=1, tiled=True)
    result = contract_last(lax.all_gather(tokens, "tensor", axis=0, tiled=True), full_rows)
    return result.astype(jnp.bfloat16)


def solution(mesh):
    placed = (P(("dp", "tensor"), None), P("tensor", "dp"))
    return jax.shard_map(
        on_device, mesh=mesh, in_specs=placed, out_specs=P("dp", "tensor"), check_vma=False
    )
```

profile of v0, /device:TPU:1, one launch (start us, length us, event | category | flops | bytes accessed | tf_op | source)
XLA Modules:
  0.0 695.2 jit_solution(15658774399451351064)
XLA Ops:
  6.5 0.0 all-gather.4.cloned.1.call-start
  6.5 0.7 all-gather.4.cloned.1.call-update
  7.3 0.0 all-gather.6.cloned.1.call-start
  7.3 86.7 %all-gather.4.cloned.1.call-done = bf16[4096,128]{1,0:T(8,128)(2,1)} async-done(((bf16[256,128]{1,0:T(8,128)(2,1)}), bf16[4096,128]{1,0:T(8,128)(2,1)}) %all-gather.4.cloned.1.call-update) | async-done | bytes 1048592 | tf_op jit(solution)/shard_map/all_gather | solution.py:20
  94.0 3.9 fusion.12
  97.9 0.0 copy-start
  97.9 0.0 copy-start.1
  97.9 255.6 %all-reduce.1 = bf16[4096,256]{1,0:T(8,128)(2,1)S(1)} all-reduce(f32[4096,256]{1,0:T(8,128)} %fusion.12), channel_id=1, replica_groups=mesh['dp'=32,'tensor'=16] {'dp'}, use_global_device_ids=true, to_apply=%region_0.0 | all-reduce | flops 1048576 | bytes 6291456 | tf_op jit(solution)/shard_map/psum | solution.py:22
  353.5 0.0 copy-done
  353.5 0.0 copy-done.1
  353.5 1.4 fusion.9
  354.9 0.0 all-gather.6.cloned.1.call-update
  354.9 0.0 all-gather.8.cloned.1.call-start
  354.9 0.7 all-gather.8.cloned.1.call-update
  355.6 193.9 %all-gather.6.cloned.1.call-done = bf16[256,4096]{1,0:T(8,128)(2,1)} async-done(((bf16[256,128]{1,0:T(8,128)(2,1)}), bf16[256,4096]{1,0:T(8,128)(2,1)}) %all-gather.6.cloned.1.call-update) | async-done | bytes 2097168 | tf_op jit(solution)/shard_map/all_gather | solution.py:25
  549.5 134.2 %all-gather.8.cloned.1.call-done = bf16[512,4096]{1,0:T(8,128)(2,1)} async-done(((bf16[32,4096]{1,0:T(8,128)(2,1)}), bf16[512,4096]{1,0:T(8,128)(2,1)}) %all-gather.8.cloned.1.call-update) | async-done | bytes 4194320 | tf_op jit(solution)/shard_map/all_gather | solution.py:26
  683.7 4.1 fusion.2
  687.9 0.8 copy.3
Async XLA Ops:
  6.5 87.5 %all-gather.4.cloned.1.call-start = ((), (), s32[]{:S(2)}) async-start(), calls=%async_computation | async-start | bytes 1114112 | tf_op jit(solution)/shard_map/all_gather | solution.py:20
  7.3 542.3 %all-gather.6.cloned.1.call-start = ((), (), s32[]{:S(2)}) async-start(), calls=%async_computation.1 | async-start | bytes 2162688 | tf_op jit(solution)/shard_map/all_gather | solution.py:25
  97.9 255.6 %copy-start = (bf16[4096,128]{1,0:T(8,128)(2,1)S(1)}, bf16[4096,128]{1,0:T(8,128)(2,1)}, u32[]{:S(2)}) copy-start(bf16[4096,128]{1,0:T(8,128)(2,1)} %all-gather.4.cloned.1.call-done) | copy-start | bytes 3145732
  97.9 255.6 %copy-start.1 = (bf16[256,128]{1,0:T(8,128)(2,1)S(1)}, bf16[256,128]{1,0:T(8,128)(2,1)}, u32[]{:S(2)}) copy-start(bf16[256,128]{1,0:T(8,128)(2,1)} %param.3) | copy-start | bytes 196612
  354.9 328.9 %all-gather.8.cloned.1.call-start = ((), (), s32[]{:S(2)}) async-start(), calls=%async_computation.2 | async-start | bytes 4456448 | tf_op jit(solution)/shard_map/all_gather | solution.py:26
Sparse Core Ops, SparseCore 0:
  10.6 83.3 all-gather.3
  355.0 194.4 all-gather.5
  552.8 130.8 all-gather.7
where the time goes:
time: 695 us
  waiting for transfers between devices  416 us (60%)
  blocking collectives  256 us (37%)
  between operations  13.1 us (2%)
  matrix products  9.36 us (1%)
    psum x1, blocking collectives, on_device(): gram_cols = lax.psum(term, 'dp').astype(jnp.bfloat16)  256 us
    all_gather x1, waiting for transfers between devices, on_device(): full_rows = lax.all_gather(ortho, 'dp', axis=1, tiled=True)  194 us
    all_gather x1, waiting for transfers between devices, on_device(): lax.all_gather(tokens, 'tensor', axis=0, tiled=True)  134 us
    all_gather x1, waiting for transfers between devices, on_device(): col_slab = lax.all_gather(weight, 'tensor', axis=0, tiled=True)  86.7 us
  transfers between devices with their start and end apart: 3, of which 3 were waited for; matrix products, arithmetic and copies ran while one was open for 0% of the time, Pallas kernels for 0%

commit v1 on v0

v1 whole, which is shorter than its diff:
```python
import functools

import jax
import jax.numpy as jnp
from jax import lax
from jax.experimental import pallas as pl
from jax.experimental.pallas import tpu as pltpu
from jax.sharding import PartitionSpec as P

MESH = pl.DeviceIdType.MESH
X, Y, H, L, C = 4, 4, 2, 8, 2
Z = H * L
B = X * H * C
LL = L // C


def dot_t(a, b):
    return lax.dot_general(a, b, (((1,), (1,)), ((), ())), preferred_element_type=jnp.float32)


def kernel(
    t_ref, w_ref, out_ref,
    zb, wc, tb, pf, pr, ys, yr, gb, ob, oc, acc,
    loc, s_z, r_z, s_x, s_w, r_w, s_p, r_p, s_y, r_y, s_g, s_h, r_g,
    s_l, r_l, s_o, s_c, s_r, r_o, s_t, s_u, r_t,
):
    dp, tn = lax.axis_index("dp"), lax.axis_index("tensor")
    y, l = lax.div(dp, L), lax.rem(dp, L)
    x, h, c = lax.div(tn, H * C), lax.rem(lax.div(tn, C), H), lax.rem(tn, C)
    z = h * L + l
    other = 1 - c
    rb, cb = w_ref.shape
    rows = t_ref.shape[0]
    cw = LL * cb
    r = rb // LL

    def dev(ax, ay, az, ac):
        return (ay * L + lax.rem(az, L), (ax * H + lax.div(az, L)) * C + ac)

    def xs(k):
        return lax.rem(x + k, X)

    def yy(k):
        return lax.rem(y + k, Y)

    def zz(k):
        return lax.rem(z + k, Z)

    def send(src, dst, ssem, rsem, device):
        return pltpu.make_async_remote_copy(
            src_ref=src, dst_ref=dst, send_sem=ssem, recv_sem=rsem, device_id=device, device_id_type=MESH
        )

    def await_copy(ref, sem):
        pltpu.make_async_copy(ref, ref, sem).wait()

    def blk(ax, ah, ac):
        return (ax * H + ah) * C + ac

    def tblk(b):
        return tb.at[pl.ds(pl.multiple_of(b * rows, rows), rows), :]

    mine = blk(x, h, c)
    load_w = pltpu.make_async_copy(w_ref, zb.at[z], loc.at[0])
    load_t = pltpu.make_async_copy(t_ref, tblk(mine), loc.at[1])
    load_w.start()
    load_t.start()

    barrier = pltpu.get_barrier_semaphore()
    peers = [dev(x, y, zz(1), c), dev(x, y, zz(Z - 1), c), dev(x, y, zz(L), c), dev(x, y, z, other)]
    peers += [dev(xs(k), y, z, a) for k in (1, X - 1) for a in (c, other)]
    peers += [dev(x, yy(k), z, a) for k in (1, Y - 1) for a in (c, other)] + [dev(x, yy(2), z, c)]
    for peer in peers:
        pl.semaphore_signal(barrier, inc=1, device_id=peer, device_id_type=MESH)
    pl.semaphore_wait(barrier, len(peers))
    load_w.wait()
    load_t.wait()

    def slot(b, k):
        return wc.at[b, :, pl.ds(pl.multiple_of(k * cb, cb), cb)]

    def up(q, i):
        send(zb.at[q], zb.at[q], s_z.at[0], r_z.at[q], dev(x, y, zz(1), c)).start()

    def down(q, i):
        send(zb.at[q], zb.at[q], s_z.at[1], r_z.at[q], dev(x, y, zz(Z - 1), c)).start()

    def spread(q):
        lq = lax.rem(q, L)
        to, k = lax.div(lq, LL), lax.rem(lq, LL)
        b = blk(x, lax.div(q, L), c)
        sem = r_w.at[b, k]
        send(zb.at[q], slot(b, k), s_x.at[0], sem, dev(xs(1), y, z, to)).start()
        send(zb.at[q], slot(b, k), s_x.at[1], sem, dev(xs(X - 1), y, z, to)).start()

        @pl.when(to != c)
        def _():
            send(zb.at[q], slot(b, k), s_x.at[2], sem, dev(x, y, z, other)).start()

        @pl.when(to == c)
        def _():
            pltpu.make_async_copy(zb.at[q], slot(b, k), sem).start()

    def relay(q):
        lq = lax.rem(q, L)
        k, hq = lax.rem(lq, LL), lax.div(q, L)

        @pl.when(lax.div(lq, LL) == c)
        def _():
            even = lax.rem(q, 2) == 0
            near = jnp.where(even, xs(X - 1), xs(1))
            far = jnp.where(even, xs(1), xs(X - 1))
            for a in range(C):
                b = blk(near, hq, a)
                await_copy(slot(b, k), r_w.at[b, k])
                send(slot(b, k), slot(b, k), s_w, r_w.at[b, k], dev(far, y, z, c)).start()

    up(z, 0)
    down(z, 0)
    spread(z)

    def z_step(s, _):
        q = zz(Z - s)
        await_copy(zb.at[q], r_z.at[q])
        up(q, s)
        p = zz(s)
        await_copy(zb.at[p], r_z.at[p])

        @pl.when(s < Z // 2 - 1)
        def _():
            down(p, s)

        spread(q)
        spread(p)

        @pl.when(s == 2)
        def _():
            relay(z)

        @pl.when(s > 2)
        def _():
            relay(zz(Z - s + 2))
            relay(zz(s - 2))

        return 0

    lax.fori_loop(1, Z // 2, z_step, 0)
    q = zz(Z // 2)
    await_copy(zb.at[q], r_z.at[q])
    spread(q)
    partner = blk(x, 1 - h, c)
    send(tblk(mine), tblk(mine), s_t.at[0], r_t.at[mine], dev(x, y, zz(L), c)).start()
    for s in (Z // 2 - 2, Z // 2 - 1):
        relay(zz(Z - s))
        relay(zz(s))
    relay(q)

    def t_spread(b):
        send(tblk(b), tblk(b), s_u.at[0], r_t.at[b], dev(xs(1), y, z, c)).start()
        send(tblk(b), tblk(b), s_u.at[1], r_t.at[b], dev(xs(X - 1), y, z, c)).start()

    def t_other(b):
        send(tblk(b), tblk(b), s_u.at[3], r_t.at[b], dev(x, y, z, other)).start()

    t_spread(mine)

    def rest(i, _):
        hq, k, a = lax.div(i, LL * C), lax.rem(lax.div(i, C), LL), lax.rem(i, C)
        q = hq * L + c * LL + k
        near = jnp.where(lax.rem(q, 2) == 0, xs(1), xs(X - 1))
        for ax in (x, xs(2), near):
            b = blk(ax, hq, a)
            await_copy(slot(b, k), r_w.at[b, k])
        return 0

    lax.fori_loop(0, H * LL * C, rest, 0)

    half = B // C
    own = blk(x, h, lax.div(l, LL))
    wr = wc[own, pl.ds(pl.multiple_of(lax.rem(l, LL) * r, r), r), :]

    def gram(i, _):
        b = lax.rem(other * half + i, B)
        pf[b] = dot_t(wr, wc[b])
        return 0

    lax.fori_loop(0, half, gram, 0)
    half_copy = send(pf.at[pl.ds(other * half, half)], pr, s_p, r_p, dev(x, y, z, other))
    half_copy.start()
    lax.fori_loop(half, B, gram, 0)
    half_copy.wait_recv()
    per = half // Y

    def fold(i, _):
        total = pf[c * half + i] + pr[i]
        pf[c * half + i] = total
        ys[i] = total.astype(jnp.bfloat16)
        return 0

    lax.fori_loop(0, half, fold, 0)
    for k in (2, 1, Y - 1):
        send(ys.at[pl.ds(yy(k) * per, per)], yr.at[k], s_y.at[k], r_y.at[k], dev(x, yy(k), z, c)).start()
    for k in (1, Y - 1, 2):
        await_copy(yr.at[k], r_y.at[k])
    for j in range(per):
        i = y * per + j
        total = pf[c * half + i]
        for k in range(1, Y):
            total = total + yr[k, j].astype(jnp.float32)
        gb[c * half + i] = total.astype(jnp.bfloat16)

    def g_at(a, k):
        return gb.at[pl.ds(a * half + k * per, per)]

    for k in (2, 1, Y - 1):
        send(g_at(c, y), g_at(c, y), s_g.at[k], r_g.at[c, y], dev(x, yy(k), z, c)).start()
    send(g_at(c, y), g_at(c, y), s_h.at[0], r_g.at[c, y], dev(x, y, z, other)).start()
    for k in (1, Y - 1, 2):
        await_copy(g_at(c, yy(k)), r_g.at[c, yy(k)])
        send(g_at(c, yy(k)), g_at(c, yy(k)), s_h.at[k], r_g.at[c, yy(k)], dev(x, y, z, other)).start()
    for k in range(Y):
        await_copy(g_at(other, yy(k)), r_g.at[other, yy(k)])

    acc_o = 1.5 * wr.astype(jnp.float32)

    def update(b, total):
        return total - 0.5 * jnp.dot(gb[b], wc[b], preferred_element_type=jnp.float32)

    ob[l] = lax.fori_loop(0, B, update, acc_o).astype(jnp.bfloat16)

    def o_slot(a, k):
        return oc.at[a, pl.ds(pl.multiple_of(k * r, r), r), :]

    def o_up(q):
        @pl.when(l < L - 1)
        def _():
            send(ob.at[q], ob.at[q], s_l.at[0, q], r_l.at[q], (dp + 1, tn)).start()

    def o_down(q):
        @pl.when(l > 0)
        def _():
            send(ob.at[q], ob.at[q], s_l.at[1, q], r_l.at[q], (dp - 1, tn)).start()

    def o_spread(q):
        to, k = lax.div(q, LL), lax.rem(q, LL)
        a = y * C + c
        send(ob.at[q], o_slot(a, k), s_o.at[0], r_o.at[a, k], dev(x, yy(1), z, to)).start()
        send(ob.at[q], o_slot(a, k), s_o.at[1], r_o.at[a, k], dev(x, yy(Y - 1), z, to)).start()

        @pl.when(to != c)
        def _():
            send(ob.at[q], o_slot(a, k), s_c, r_o.at[a, k], dev(x, y, z, other)).start()

        @pl.when(to == c)
        def _():
            pltpu.make_async_copy(ob.at[q], o_slot(a, k), r_o.at[a, k]).start()

    def o_relay(q):
        @pl.when(lax.div(q, LL) == c)
        def _():
            k = lax.rem(q, LL)
            for a, near, far in ((yy(Y - 1) * C, yy(Y - 1), yy(1)), (yy(1) * C + 1, yy(1), yy(Y - 1))):
                await_copy(o_slot(a, k), r_o.at[a, k])
                send(o_slot(a, k), o_slot(a, k), s_r, r_o.at[a, k], dev(x, far, z, c)).start()

    o_up(l)
    o_down(l)
    o_spread(l)

    await_copy(tblk(partner), r_t.at[partner])
    t_spread(partner)
    t_other(mine)
    t_other(partner)

    def l_step(s, _):
        @pl.when(l - s >= 0)
        def _():
            await_copy(ob.at[l - s], r_l.at[l - s])
            o_up(l - s)
            o_spread(l - s)

        @pl.when(l + s < L)
        def _():
            await_copy(ob.at[l + s], r_l.at[l + s])
            o_down(l + s)
            o_spread(l + s)

        @pl.when(s == 2)
        def _():
            o_relay(l)

        @pl.when((s > 2) & (l - s + 2 >= 0))
        def _():
            o_relay(l - s + 2)

        @pl.when((s > 2) & (l + s - 2 < L))
        def _():
            o_relay(l + s - 2)

        return 0

    lax.fori_loop(1, L, l_step, 0)

    for hq, near, far in ((0, xs(X - 1), xs(1)), (1, xs(1), xs(X - 1))):
        b = blk(near, hq, c)
        await_copy(tblk(b), r_t.at[b])
        send(tblk(b), tblk(b), s_u.at[2], r_t.at[b], dev(far, y, z, c)).start()
        t_other(b)
    for hq, near in ((1, xs(X - 1)), (0, xs(1))):
        b = blk(near, hq, c)
        await_copy(tblk(b), r_t.at[b])
        t_other(b)

    for s in (L - 2, L - 1):
        @pl.when(l - s >= 0)
        def _():
            o_relay(l - s)

        @pl.when(l + s < L)
        def _():
            o_relay(l + s)

    for hq in range(H):
        b = blk(xs(2), hq, c)
        await_copy(tblk(b), r_t.at[b])
        t_other(b)
    for k in range(X):
        for hq in range(H):
            b = blk(xs(k), hq, other)
            await_copy(tblk(b), r_t.at[b])

    def o_rest(k, _):
        for a in (y * C, y * C + 1, yy(2) * C, yy(2) * C + 1, yy(Y - 1) * C + 1, yy(1) * C):
            await_copy(o_slot(a, k), r_o.at[a, k])
        return 0

    lax.fori_loop(0, LL, o_rest, 0)

    acc[...] = jnp.zeros_like(acc)

    def project(a, _):
        acc[...] += dot_t(tb[:, pl.ds(pl.multiple_of(a * cw, cw), cw)], oc[a])
        return 0

    lax.fori_loop(0, Y * C, project, 0)
    out_ref[...] = acc[...].astype(jnp.bfloat16)

    def sent(ref, sem):
        pltpu.make_async_copy(ref, ref, sem).wait()

    sent(zb.at[pl.ds(0, Z // 2)], s_z.at[0])
    sent(zb.at[pl.ds(0, Z // 2 - 1)], s_z.at[1])
    sent(zb, s_x.at[0])
    sent(zb, s_x.at[1])
    sent(zb.at[pl.ds(0, Z // 2)], s_x.at[2])
    sent(zb, s_w)
    half_copy.wait_send()
    for k in range(1, Y):
        sent(yr.at[k], s_y.at[k])
        sent(yr.at[k], s_g.at[k])
    for k in range(Y):
        sent(yr.at[0], s_h.at[k])
    sent(tblk(mine), s_t.at[0])
    two, eight = tb.at[pl.ds(0, H * rows), :], tb.at[pl.ds(0, X * H * rows), :]
    sent(two, s_u.at[0])
    sent(two, s_u.at[1])
    sent(two, s_u.at[2])
    sent(eight, s_u.at[3])
    sent(ob, s_o.at[0])
    sent(ob, s_o.at[1])
    sent(ob.at[pl.ds(0, L // 2)], s_c)
    sent(ob, s_r)

    def line(q, _):
        @pl.when((l < L - 1) & (q <= l))
        def _():
            sent(ob.at[q], s_l.at[0, q])

        @pl.when((l > 0) & (q >= l))
        def _():
            sent(ob.at[q], s_l.at[1, q])

        return 0

    lax.fori_loop(0, L, line, 0)


def on_device(tokens, weight):
    rows, d = tokens.shape
    rb, cb = weight.shape
    cw, r, half = LL * cb, rb // LL, B // C
    dma = pltpu.SemaphoreType.DMA
    bf, f32 = jnp.bfloat16, jnp.float32
    return pl.pallas_call(
        kernel,
        out_shape=jax.ShapeDtypeStruct((B * rows, rb), bf),
        in_specs=[pl.BlockSpec(memory_space=pl.ANY)] * 2,
        out_specs=pl.BlockSpec(memory_space=pltpu.VMEM),
        scratch_shapes=[
            pltpu.VMEM((Z, rb, cb), bf),
            pltpu.VMEM((B, rb, cw), bf),
            pltpu.VMEM((B * rows, d), bf),
            pltpu.VMEM((B, r, rb), f32),
            pltpu.VMEM((half, r, rb), f32),
            pltpu.VMEM((half, r, rb), bf),
            pltpu.VMEM((Y, half // Y, r, rb), bf),
            pltpu.VMEM((B, r, rb), bf),
            pltpu.VMEM((L, r, cw), bf),
            pltpu.VMEM((Y * C, rb, cw), bf),
            pltpu.VMEM((B * rows, rb), f32),
            dma((2,)),
            dma((2,)), dma((Z,)), dma((3,)), dma, dma((B, LL)),
            dma, dma, dma((Y,)), dma((Y,)), dma((Y,)), dma((Y,)), dma((C, Y)),
            dma((2, L)), dma((L,)), dma((2,)), dma, dma, dma((Y * C, LL)),
            dma((1,)), dma((4,)), dma((B,)),
        ],
        compiler_params=pltpu.CompilerParams(
            collective_id=0, has_side_effects=True, vmem_limit_bytes=48 * 1024 * 1024
        ),
        name="bjorck",
    )(tokens, weight)


def solution(mesh):
    placed = (P(("dp", "tensor"), None), P("tensor", "dp"))
    return jax.shard_map(
        on_device, mesh=mesh, in_specs=placed, out_specs=P("dp", "tensor"), check_vma=False
    )
```

time: 695 us -> 123 us (0.18)
  waiting for transfers between devices: 416 us -> 0 us
  blocking collectives: 256 us -> 0 us
  Pallas kernels: 0 us -> 120 us
  between operations: 13.1 us -> 0.01 us
  matrix products: 9.36 us -> 0 us
    all_gather x3 -> x0, waiting for transfers between devices: 415 us -> none  [the longest x1 194 us: on_device(): full_rows = lax.all_gather(ortho, 'dp', axis=1, tiled=True)]
    psum x1 -> x0, blocking collectives: 256 us -> none  [on_device(): gram_cols = lax.psum(term, 'dp').astype(jnp.bfloat16)]
    pallas_call x0 -> x1, Pallas kernels: none -> 120 us  [on_device(): pl.pallas_call(kernel, out_shape=jax.ShapeDtypeStruct((B * rows, rb), bf)...]
    dot_general x3 -> x0, matrix products: 9.36 us -> none  [the longest x2 7.98 us: contract_last(): lax.dot_general(left, right, (((1,), (1,)), ((), ())), preferred_element_...]
  transfers between devices with their start and end apart: 3 -> 0, of which waited for: 3 -> 0; matrix products, arithmetic and copies ran while one was open for 0% -> 0% of each run, Pallas kernels for 0% -> 0%
where the time goes in v1:
time: 123 us; the launch traced here: 122 us
  Pallas kernels  120 us (98%)
  local copies, waits for them, and re-layouts  2.49 us (2%)
    pallas_call x1, Pallas kernels, on_device(): pl.pallas_call(kernel, out_shape=jax.ShapeDtypeStruct((B * rows, rb), bf)...  120 us
    unnamed x5, local copies, waits for them, and re-layouts  2.49 us

profile of v1, /device:TPU:1, one launch (start us, length us, event | category | flops | bytes accessed | tf_op | source)
XLA Modules:
  0.0 122.4 jit_solution(4202133088369406619)
XLA Ops:
  0.0 0.0 copy-start
  0.0 0.9 copy-done
  1.0 0.0 copy-start.1
  1.0 0.8 copy-done.1
  1.8 119.9 %bjorck.1 = bf16[512,256]{1,0:T(8,128)(2,1)S(1)} custom-call(bf16[32,4096]{1,0:T(8,128)(2,1)S(1)} %copy-done, bf16[256,128]{1,0:T(8,128)(2,1)S(1)} %copy-done.1), custom_call_target="tpu_custom_call" | custom-call | tf_op jit(solution)/shard_map/bjorck/pallas_call | solution.py:394
  121.7 0.7 copy.4
Async XLA Ops:
  0.0 0.9 copy-start
  1.0 0.8 copy-start.1

commit v2 on v1

v2 whole, which is shorter than its diff:
```python
import functools

import jax
import jax.numpy as jnp
from jax import lax
from jax.experimental import pallas as pl
from jax.experimental.pallas import tpu as pltpu
from jax.sharding import PartitionSpec as P

MESH = pl.DeviceIdType.MESH
X, Y, H, L, C = 4, 4, 2, 8, 2
Z = H * L
B = X * H * C
LL = L // C
NC, FC = 2, 2


def dot_t(a, b):
    return lax.dot_general(a, b, (((1,), (1,)), ((), ())), preferred_element_type=jnp.float32)


def kernel(
    t_ref, w_ref, out_ref,
    zb, wc, rr, tb, t4, pf, pr, ys, yr, gb, po, xb, xr, ob, oc, acc,
    loc, s_z, r_z, s_x, s_m, r_m, r_w, s_p, r_p, s_y, r_y, s_g, s_h, r_g, s_q, r_q,
    s_l, r_l, s_o, s_c, s_r, r_o, s_t, r_t4, r_tp, s_u, r_t,
):
    dp, tn = lax.axis_index("dp"), lax.axis_index("tensor")
    y, l = lax.div(dp, L), lax.rem(dp, L)
    x, h, c = lax.div(tn, H * C), lax.rem(lax.div(tn, C), H), lax.rem(tn, C)
    z = h * L + l
    other = 1 - c
    rb, cb = w_ref.shape
    rows = t_ref.shape[0]
    cw = LL * cb
    r = rb // LL
    zr, fr, tr = rb // NC, r // FC, rows // 2

    def dev(ax, ay, az, ac):
        return (ay * L + lax.rem(az, L), (ax * H + lax.div(az, L)) * C + ac)

    def xs(k):
        return lax.rem(x + k, X)

    def yy(k):
        return lax.rem(y + k, Y)

    def zz(k):
        return lax.rem(z + k, Z)

    def send(src, dst, ssem, rsem, device):
        return pltpu.make_async_remote_copy(
            src_ref=src, dst_ref=dst, send_sem=ssem, recv_sem=rsem, device_id=device, device_id_type=MESH
        )

    def await_copy(ref, sem):
        pltpu.make_async_copy(ref, ref, sem).wait()

    def blk(ax, ah, ac):
        return (ax * H + ah) * C + ac

    def tblk(b):
        return tb.at[pl.ds(pl.multiple_of(b * rows, rows), rows), :]

    def thalf(b, i):
        return tb.at[pl.ds(pl.multiple_of(b * rows + i * tr, tr), tr), :]

    def part(ref, i):
        return ref.at[pl.ds(pl.multiple_of(i * r, r), r), :]

    mine, partner = blk(x, h, c), blk(x, 1 - h, c)
    loads = [pltpu.make_async_copy(w_ref.at[pl.ds(i * zr, zr), :], zb.at[z, i], loc.at[i]) for i in range(NC)]
    loads.append(pltpu.make_async_copy(t_ref, tblk(mine), loc.at[NC]))
    for load in loads:
        load.start()

    barrier = pltpu.get_barrier_semaphore()
    peers = [dev(x, y, zz(1), c), dev(x, y, zz(Z - 1), c), dev(x, y, z, other)]
    peers += [dev(xs(k), y, z, a) for k in (1, 2, 3) for a in (c, other)]
    peers += [dev(x, yy(k), z, a) for k in (1, Y - 1) for a in (c, other)] + [dev(x, yy(2), z, c)]
    for peer in peers:
        pl.semaphore_signal(barrier, inc=1, device_id=peer, device_id_type=MESH)
    pl.semaphore_wait(barrier, len(peers))
    for load in loads:
        load.wait()

    own_core, own_row = lax.div(l, LL), lax.rem(l, LL) * r
    own_chunk = lax.div(own_row, zr)

    def slot(b, i, k):
        return wc.at[b, pl.ds(i * zr, zr), pl.ds(pl.multiple_of(k * cb, cb), cb)]

    def up(q, i, sem=0):
        send(zb.at[q, i], zb.at[q, i], s_z.at[sem], r_z.at[q, i], dev(x, y, zz(1), c)).start()

    def down(q, i, sem=1):
        send(zb.at[q, i], zb.at[q, i], s_z.at[sem], r_z.at[q, i], dev(x, y, zz(Z - 1), c)).start()

    def spread(q, i):
        lq, hq = lax.rem(q, L), lax.div(q, L)
        to, k = lax.div(lq, LL), lax.rem(lq, LL)
        b = hq * C + c

        @pl.when((hq == h) & (own_core == c) & (own_chunk == i))
        def _():
            src = zb.at[q, i, pl.ds(pl.multiple_of(own_row - i * zr, r), r), :]
            dst = rr.at[pl.ds(pl.multiple_of(x * r, r), r), pl.ds(pl.multiple_of(k * cb, cb), cb)]
            for n in (2, 1, 3):
                send(src, dst, s_m, r_m.at[x, k], dev(xs(n), y, z, to)).start()

        @pl.when(to != c)
        def _():
            send(zb.at[q, i], slot(b, i, k), s_x, r_w.at[b, i, k], dev(x, y, z, other)).start()

        @pl.when(to == c)
        def _():
            pltpu.make_async_copy(zb.at[q, i], slot(b, i, k), r_w.at[b, i, k]).start()
    for i in range(NC):
        up(z, i)
        down(z, i)
    for i in range(NC):
        spread(z, i)

    def z_step(s, _):
        q, p = zz(Z - s), zz(s)
        for i in range(NC):
            await_copy(zb.at[q, i], r_z.at[q, i])
            up(q, i)
            await_copy(zb.at[p, i], r_z.at[p, i])
            down(p, i)
        for i in range(NC):
            spread(q, i)
            spread(p, i)
        return 0
    lax.fori_loop(1, Z // 2 - 1, z_step, 0)
    q, p = zz(Z // 2 + 1), zz(Z // 2 - 1)
    for i in range(NC):
        await_copy(zb.at[q, i], r_z.at[q, i])
        if i < NC // 2:
            up(q, i, 2)
        await_copy(zb.at[p, i], r_z.at[p, i])
        if i >= NC // 2:
            down(p, i, 3)
    for i in range(NC):
        spread(q, i)
        spread(p, i)

    def t_spread(b):
        send(tblk(b), tblk(b), s_u.at[0], r_t.at[b], dev(xs(1), y, z, c)).start()
        send(tblk(b), tblk(b), s_u.at[1], r_t.at[b], dev(xs(X - 1), y, z, c)).start()

    def t_other(b):
        send(tblk(b), tblk(b), s_u.at[3], r_t.at[b], dev(x, y, z, other)).start()

    quarter = Z // 4
    q = zz(Z // 2)
    for i in range(NC):
        await_copy(zb.at[q, i], r_z.at[q, i])
        spread(q, i)
    send(thalf(mine, 0), t4.at[0], s_t.at[0], r_t4.at[0], dev(x, y, zz(quarter), c)).start()
    send(thalf(mine, 1), t4.at[1], s_t.at[1], r_t4.at[1], dev(x, y, zz(Z - quarter), c)).start()
    for b in range(H * C):
        for i in range(NC):
            for k in range(LL):
                await_copy(slot(b, i, k), r_w.at[b, i, k])
    for n in (1, 2, 3):
        for k in range(LL):
            await_copy(
                rr.at[pl.ds(pl.multiple_of(xs(n) * r, r), r), pl.ds(k * cb, cb)], r_m.at[xs(n), k]
            )
    t_spread(mine)
    t_other(mine)

    half = H * C // C
    wr = wc[h * C + own_core, pl.ds(pl.multiple_of(own_row, r), r), :]
    rr[pl.ds(pl.multiple_of(x * r, r), r), :] = wr
    for i in range(half):
        b = other * half + i
        pf[b] = dot_t(rr[...], wc[b])
    half_copy = send(pf.at[pl.ds(other * half, half)], pr, s_p, r_p, dev(x, y, z, other))
    half_copy.start()
    for i in range(half):
        b = c * half + i
        pf[b] = dot_t(rr[...], wc[b])
    half_copy.wait_recv()
    for i in range(half):
        total = pf[c * half + i] + pr[i]
        pf[c * half + i] = total
        ys[i] = total.astype(jnp.bfloat16)

    def y_part(ref, k):
        return ref.at[:, pl.ds(pl.multiple_of(k * r, r), r), :]

    for k in (2, 1, Y - 1):
        send(y_part(ys, yy(k)), yr.at[k], s_y.at[k], r_y.at[k], dev(x, yy(k), z, c)).start()
    for k in (1, Y - 1, 2):
        await_copy(yr.at[k], r_y.at[k])
    my_rows = pl.ds(pl.multiple_of(y * r, r), r)
    for i in range(half):
        total = pf[c * half + i, my_rows, :]
        for k in range(1, Y):
            total = total + yr[k, i].astype(jnp.float32)
        gb[c * half + i, my_rows, :] = total.astype(jnp.bfloat16)

    def g_at(a, k):
        return gb.at[pl.ds(a * half, half), pl.ds(pl.multiple_of(k * r, r), r), :]
    for k in (2, 1, Y - 1):
        send(g_at(c, y), g_at(c, y), s_g.at[k], r_g.at[c, y], dev(x, yy(k), z, c)).start()
    send(g_at(c, y), g_at(c, y), s_h.at[0], r_g.at[c, y], dev(x, y, z, other)).start()
    for k in (1, Y - 1, 2):
        await_copy(g_at(c, yy(k)), r_g.at[c, yy(k)])
        send(g_at(c, yy(k)), g_at(c, yy(k)), s_h.at[k], r_g.at[c, yy(k)], dev(x, y, z, other)).start()
    for i, ahead, back in ((0, quarter, Z - quarter), (1, Z - quarter, quarter)):
        await_copy(t4.at[i], r_t4.at[i])
        home = blk(x, lax.div(zz(back), L), c)
        send(t4.at[i], thalf(home, i), s_t.at[2 + i], r_tp.at[i], dev(x, y, zz(ahead), c)).start()
    for k in range(Y):
        await_copy(g_at(other, yy(k)), r_g.at[other, yy(k)])

    total = jnp.dot(gb[0], wc[0], preferred_element_type=jnp.float32)
    for b in range(1, H * C):
        total = total + jnp.dot(gb[b], wc[b], preferred_element_type=jnp.float32)
    total = -0.5 * total
    po[...] = total
    xb[...] = total.astype(jnp.bfloat16)
    for n in (2, 1, 3):
        send(part(xb, xs(n)), xr.at[n], s_q.at[n], r_q.at[n], dev(xs(n), y, z, c)).start()
    for n in (1, 3, 2):
        await_copy(xr.at[n], r_q.at[n])
    total = 1.5 * wr.astype(jnp.float32) + po[pl.ds(pl.multiple_of(x * r, r), r), :]
    for n in (1, 2, 3):
        total = total + xr[n].astype(jnp.float32)
    for i in range(FC):
        ob[l, i] = total[i * fr:(i + 1) * fr].astype(jnp.bfloat16)

    def o_slot(a, k, i):
        return oc.at[a, pl.ds(pl.multiple_of(k * r + i * fr, fr), fr), :]

    def o_up(q, i):
        @pl.when(l < L - 1)
        def _():
            send(ob.at[q, i], ob.at[q, i], s_l.at[0, q], r_l.at[q, i], (dp + 1, tn)).start()

    def o_down(q, i):
        @pl.when(l > 0)
        def _():
            send(ob.at[q, i], ob.at[q, i], s_l.at[1, q], r_l.at[q, i], (dp - 1, tn)).start()

    def o_spread(q, i):
        to, k = lax.div(q, LL), lax.rem(q, LL)
        a = y * C + c
        dst, sem = o_slot(a, k, i), r_o.at[a, k, i]
        send(ob.at[q, i], dst, s_o.at[0], sem, dev(x, yy(1), z, to)).start()
        send(ob.at[q, i], dst, s_o.at[1], sem, dev(x, yy(Y - 1), z, to)).start()

        @pl.when(to != c)
        def _():
            send(ob.at[q, i], dst, s_c, sem, dev(x, y, z, other)).start()

        @pl.when(to == c)
        def _():
            pltpu.make_async_copy(ob.at[q, i], dst, sem).start()

    def o_relay(q):
        @pl.when(lax.div(q, LL) == c)
        def _():
            k = lax.rem(q, LL)
            for i in range(FC):
                for a, far in ((yy(Y - 1) * C, yy(1)), (yy(1) * C + 1, yy(Y - 1))):
                    await_copy(o_slot(a, k, i), r_o.at[a, k, i])
                    send(o_slot(a, k, i), o_slot(a, k, i), s_r, r_o.at[a, k, i], dev(x, far, z, c)).start()
    for i in range(FC):
        o_up(l, i)
        o_down(l, i)
    for i in range(FC):
        o_spread(l, i)

    def t_pass(hq, a, b):
        near = blk(a, hq, c)
        await_copy(tblk(near), r_t.at[near])
        send(tblk(near), tblk(near), s_u.at[2], r_t.at[near], dev(b, y, z, c)).start()
        t_other(near)

    def t_turn(hq):
        @pl.when(hq == 0)
        def _():
            t_pass(0, xs(X - 1), xs(1))

        @pl.when(hq == 1)
        def _():
            t_pass(1, xs(1), xs(X - 1))
    t_turn(h)

    def l_step(s, _):
        for i in range(FC):
            @pl.when(l - s >= 0)
            def _():
                await_copy(ob.at[l - s, i], r_l.at[l - s, i])
                o_up(l - s, i)

            @pl.when(l + s < L)
            def _():
                await_copy(ob.at[l + s, i], r_l.at[l + s, i])
                o_down(l + s, i)

        for i in range(FC):
            @pl.when(l - s >= 0)
            def _():
                o_spread(l - s, i)

            @pl.when(l + s < L)
            def _():
                o_spread(l + s, i)

        @pl.when(s == 2)
        def _():
            o_relay(l)

        @pl.when((s > 2) & (l - s + 2 >= 0))
        def _():
            o_relay(l - s + 2)

        @pl.when((s > 2) & (l + s - 2 < L))
        def _():
            o_relay(l + s - 2)

        @pl.when(s == 2)
        def _():
            await_copy(thalf(partner, 0), r_tp.at[0])
            await_copy(thalf(partner, 1), r_tp.at[1])
            t_spread(partner)
            t_other(partner)

        @pl.when(s == 5)
        def _():
            t_turn(1 - h)

        return 0
    lax.fori_loop(1, L, l_step, 0)
    for s in (L - 2, L - 1):
        @pl.when(l - s >= 0)
        def _():
            o_relay(l - s)

        @pl.when(l + s < L)
        def _():
            o_relay(l + s)
    for hq, a in ((1, xs(X - 1)), (0, xs(1)), (0, xs(2)), (1, xs(2))):
        b = blk(a, hq, c)
        await_copy(tblk(b), r_t.at[b])
        t_other(b)
    for k in range(X):
        for hq in range(H):
            b = blk(xs(k), hq, other)
            await_copy(tblk(b), r_t.at[b])

    def o_rest(k, _):
        for i in range(FC):
            for a in (y * C, y * C + 1, yy(2) * C, yy(2) * C + 1, yy(Y - 1) * C + 1, yy(1) * C):
                await_copy(o_slot(a, k, i), r_o.at[a, k, i])
        return 0
    lax.fori_loop(0, LL, o_rest, 0)
    acc[...] = jnp.zeros_like(acc)

    def project(a, _):
        acc[...] += dot_t(tb[:, pl.ds(pl.multiple_of(a * cw, cw), cw)], oc[a])
        return 0

    lax.fori_loop(0, Y * C, project, 0)
    out_ref[...] = acc[...].astype(jnp.bfloat16)

    def sent(ref, sem):
        pltpu.make_async_copy(ref, ref, sem).wait()
    for n in range(2):
        sent(zb.at[pl.ds(0, Z // 2 - 1)], s_z.at[n])
        sent(zb.at[0, pl.ds(0, NC // 2)], s_z.at[2 + n])
    sent(zb.at[pl.ds(0, Z // 2)], s_x)

    @pl.when(own_core == c)
    def _():
        sent(zb.at[pl.ds(0, L * 3 // LL)], s_m)

    half_copy.wait_send()
    for k in range(1, Y):
        sent(yr.at[k], s_y.at[k])
        sent(yr.at[k], s_g.at[k])
        sent(xr.at[k], s_q.at[k])
    for k in range(Y):
        sent(yr.at[0], s_h.at[k])
    for k in range(4):
        sent(t4.at[0], s_t.at[k])
    two, eight = tb.at[pl.ds(0, H * rows), :], tb.at[pl.ds(0, X * H * rows), :]
    sent(two, s_u.at[0])
    sent(two, s_u.at[1])
    sent(two, s_u.at[2])
    sent(eight, s_u.at[3])
    sent(ob, s_o.at[0])
    sent(ob, s_o.at[1])
    sent(ob.at[pl.ds(0, L // 2)], s_c)
    sent(ob, s_r)

    def line(q, _):
        @pl.when((l < L - 1) & (q <= l))
        def _():
            sent(ob.at[q], s_l.at[0, q])

        @pl.when((l > 0) & (q >= l))
        def _():
            sent(ob.at[q], s_l.at[1, q])

        return 0

    lax.fori_loop(0, L, line, 0)


def on_device(tokens, weight):
    rows, d = tokens.shape
    rb, cb = weight.shape
    cw, r, half = LL * cb, rb // LL, H
    dma = pltpu.SemaphoreType.DMA
    bf, f32 = jnp.bfloat16, jnp.float32
    return pl.pallas_call(
        kernel,
        out_shape=jax.ShapeDtypeStruct((B * rows, rb), bf),
        in_specs=[pl.BlockSpec(memory_space=pl.ANY)] * 2,
        out_specs=pl.BlockSpec(memory_space=pltpu.VMEM),
        scratch_shapes=[
            pltpu.VMEM((Z, NC, rb // NC, cb), bf),
            pltpu.VMEM((H * C, rb, cw), bf),
            pltpu.VMEM((X * r, cw), bf),
            pltpu.VMEM((B * rows, d), bf),
            pltpu.VMEM((2, rows // 2, d), bf),
            pltpu.VMEM((H * C, X * r, rb), f32),
            pltpu.VMEM((half, X * r, rb), f32),
            pltpu.VMEM((half, X * r, rb), bf),
            pltpu.VMEM((Y, half, r, rb), bf),
            pltpu.VMEM((H * C, X * r, rb), bf),
            pltpu.VMEM((X * r, cw), f32),
            pltpu.VMEM((X * r, cw), bf),
            pltpu.VMEM((X, r, cw), bf),
            pltpu.VMEM((L, FC, r // FC, cw), bf),
            pltpu.VMEM((Y * C, rb, cw), bf),
            pltpu.VMEM((B * rows, rb), f32),
            dma((NC + 1,)),
            dma((4,)), dma((Z, NC)), dma, dma, dma((X, LL)), dma((H * C, NC, LL)),
            dma, dma, dma((Y,)), dma((Y,)), dma((Y,)), dma((Y,)), dma((C, Y)), dma((X,)), dma((X,)),
            dma((2, L)), dma((L, FC)), dma((2,)), dma, dma, dma((Y * C, LL, FC)),
            dma((4,)), dma((2,)), dma((2,)), dma((4,)), dma((B,)),
        ],
        compiler_params=pltpu.CompilerParams(
            collective_id=0, has_side_effects=True, vmem_limit_bytes=64_000_000
        ),
        name="bjorck",
    )(tokens, weight)


def solution(mesh):
    placed = (P(("dp", "tensor"), None), P("tensor", "dp"))
    return jax.shard_map(
        on_device, mesh=mesh, in_specs=placed, out_specs=P("dp", "tensor"), check_vma=False
    )
```

time: 123 us -> 102 us (0.83)
  Pallas kernels: 120 us -> 99.9 us
    pallas_call x1, Pallas kernels: 120 us -> 99.9 us  [on_device(): pl.pallas_call(kernel, out_shape=jax.ShapeDtypeStruct((B * rows, rb), bf)...]
    unnamed x5 -> x1, local copies, waits for them, and re-layouts: 2.49 us -> 1.67 us
where the time goes in v2:
time: 102 us
  Pallas kernels  99.9 us (98%)
  local copies, waits for them, and re-layouts  1.67 us (2%)
    pallas_call x1, Pallas kernels, on_device(): pl.pallas_call(kernel, out_shape=jax.ShapeDtypeStruct((B * rows, rb), bf)...  99.9 us

profile of v2, /device:TPU:1, one launch (start us, length us, event | category | flops | bytes accessed | tf_op | source)
XLA Modules:
  0.0 101.6 jit_solution(4432537541616803318)
XLA Ops:
  0.0 99.9 %bjorck.1 = bf16[512,256]{1,0:T(8,128)(2,1)} custom-call(bf16[32,4096]{1,0:T(8,128)(2,1)} %t_ref.1, bf16[256,128]{1,0:T(8,128)(2,1)} %w_ref.1), custom_call_target="tpu_custom_call" | custom-call | tf_op jit(solution)/shard_map/bjorck/pallas_call | solution.py:422
  99.9 1.7 %copy.4 = bf16[512,256]{1,0:T(8,128)(2,1)} copy(bf16[512,256]{1,0:T(8,128)(2,1)} %bjorck.1) | data formatting | bytes 524288

commit v3 on v2

--- a/solution.py
+++ b/solution.py
@@ -12,7 +12,7 @@
 Z = H * L
 B = X * H * C
 LL = L // C
-NC, FC = 2, 2
+NC, FC = 4, 4
 
 
 def dot_t(a, b):
@@ -115,11 +115,35 @@
         @pl.when(to == c)
         def _():
             pltpu.make_async_copy(zb.at[q, i], slot(b, i, k), r_w.at[b, i, k]).start()
+
+    def t_spread(b):
+        send(tblk(b), tblk(b), s_u.at[0], r_t.at[b], dev(xs(1), y, z, c)).start()
+        send(tblk(b), tblk(b), s_u.at[1], r_t.at[b], dev(xs(X - 1), y, z, c)).start()
+
+    def t_other(b):
+        send(tblk(b), tblk(b), s_u.at[3], r_t.at[b], dev(x, y, z, other)).start()
+
+    def t_pass(hq, a, b):
+        near = blk(a, hq, c)
+        await_copy(tblk(near), r_t.at[near])
+        send(tblk(near), tblk(near), s_u.at[2], r_t.at[near], dev(b, y, z, c)).start()
+        t_other(near)
+
+    def t_turn(hq):
+        @pl.when(hq == 0)
+        def _():
+            t_pass(0, xs(X - 1), xs(1))
+
+        @pl.when(hq == 1)
+        def _():
+            t_pass(1, xs(1), xs(X - 1))
     for i in range(NC):
         up(z, i)
         down(z, i)
     for i in range(NC):
         spread(z, i)
+    t_spread(mine)
+    t_other(mine)
 
     def z_step(s, _):
         q, p = zz(Z - s), zz(s)
@@ -145,20 +169,14 @@
         spread(q, i)
         spread(p, i)
 
-    def t_spread(b):
-        send(tblk(b), tblk(b), s_u.at[0], r_t.at[b], dev(xs(1), y, z, c)).start()
-        send(tblk(b), tblk(b), s_u.at[1], r_t.at[b], dev(xs(X - 1), y, z, c)).start()
-
-    def t_other(b):
-        send(tblk(b), tblk(b), s_u.at[3], r_t.at[b], dev(x, y, z, other)).start()
-
     quarter = Z // 4
+    send(thalf(mine, 0), t4.at[0], s_t.at[0], r_t4.at[0], dev(x, y, zz(quarter), c)).start()
+    send(thalf(mine, 1), t4.at[1], s_t.at[1], r_t4.at[1], dev(x, y, zz(Z - quarter), c)).start()
+    t_turn(h)
     q = zz(Z // 2)
     for i in range(NC):
         await_copy(zb.at[q, i], r_z.at[q, i])
         spread(q, i)
-    send(thalf(mine, 0), t4.at[0], s_t.at[0], r_t4.at[0], dev(x, y, zz(quarter), c)).start()
-    send(thalf(mine, 1), t4.at[1], s_t.at[1], r_t4.at[1], dev(x, y, zz(Z - quarter), c)).start()
     for b in range(H * C):
         for i in range(NC):
             for k in range(LL):
@@ -168,8 +186,6 @@
             await_copy(
                 rr.at[pl.ds(pl.multiple_of(xs(n) * r, r), r), pl.ds(k * cb, cb)], r_m.at[xs(n), k]
             )
-    t_spread(mine)
-    t_other(mine)
 
     half = H * C // C
     wr = wc[h * C + own_core, pl.ds(pl.multiple_of(own_row, r), r), :]
@@ -196,6 +212,10 @@
     for k in (1, Y - 1, 2):
         await_copy(yr.at[k], r_y.at[k])
     my_rows = pl.ds(pl.multiple_of(y * r, r), r)
+    for i, ahead, back in ((0, quarter, Z - quarter), (1, Z - quarter, quarter)):
+        await_copy(t4.at[i], r_t4.at[i])
+        home = blk(x, lax.div(zz(back), L), c)
+        send(t4.at[i], thalf(home, i), s_t.at[2 + i], r_tp.at[i], dev(x, y, zz(ahead), c)).start()
     for i in range(half):
         total = pf[c * half + i, my_rows, :]
         for k in range(1, Y):
@@ -210,10 +230,6 @@
     for k in (1, Y - 1, 2):
         await_copy(g_at(c, yy(k)), r_g.at[c, yy(k)])
         send(g_at(c, yy(k)), g_at(c, yy(k)), s_h.at[k], r_g.at[c, yy(k)], dev(x, y, z, other)).start()
-    for i, ahead, back in ((0, quarter, Z - quarter), (1, Z - quarter, quarter)):
-        await_copy(t4.at[i], r_t4.at[i])
-        home = blk(x, lax.div(zz(back), L), c)
-        send(t4.at[i], thalf(home, i), s_t.at[2 + i], r_tp.at[i], dev(x, y, zz(ahead), c)).start()
     for k in range(Y):
         await_copy(g_at(other, yy(k)), r_g.at[other, yy(k)])
 
@@ -275,22 +291,6 @@
     for i in range(FC):
         o_spread(l, i)
 
-    def t_pass(hq, a, b):
-        near = blk(a, hq, c)
-        await_copy(tblk(near), r_t.at[near])
-        send(tblk(near), tblk(near), s_u.at[2], r_t.at[near], dev(b, y, z, c)).start()
-        t_other(near)
-
-    def t_turn(hq):
-        @pl.when(hq == 0)
-        def _():
-            t_pass(0, xs(X - 1), xs(1))
-
-        @pl.when(hq == 1)
-        def _():
-            t_pass(1, xs(1), xs(X - 1))
-    t_turn(h)
-
     def l_step(s, _):
         for i in range(FC):
             @pl.when(l - s >= 0)
@@ -324,14 +324,14 @@
         def _():
             o_relay(l + s - 2)
 
-        @pl.when(s == 2)
+        @pl.when(s == 1)
         def _():
             await_copy(thalf(partner, 0), r_tp.at[0])
             await_copy(thalf(partner, 1), r_tp.at[1])
             t_spread(partner)
             t_other(partner)
 
-        @pl.when(s == 5)
+        @pl.when(s == 4)
         def _():
             t_turn(1 - h)
 
@@ -354,19 +354,23 @@
             b = blk(xs(k), hq, other)
             await_copy(tblk(b), r_t.at[b])
 
-    def o_rest(k, _):
-        for i in range(FC):
-            for a in (y * C, y * C + 1, yy(2) * C, yy(2) * C + 1, yy(Y - 1) * C + 1, yy(1) * C):
+    acc[...] = jnp.zeros_like(acc)
+
+    def take(a):
+        for k in range(LL):
+            for i in range(FC):
                 await_copy(o_slot(a, k, i), r_o.at[a, k, i])
-        return 0
-    lax.fori_loop(0, LL, o_rest, 0)
-    acc[...] = jnp.zeros_like(acc)
-
-    def project(a, _):
+
+    def project(i, first):
+        a = lax.rem(first + i, Y * C)
         acc[...] += dot_t(tb[:, pl.ds(pl.multiple_of(a * cw, cw), cw)], oc[a])
-        return 0
-
-    lax.fori_loop(0, Y * C, project, 0)
+        return first
+    for a in (y * C, y * C + 1, yy(Y - 1) * C + 1, yy(1) * C):
+        take(a)
+    lax.fori_loop(0, 3 * C, project, yy(Y - 1) * C)
+    take(yy(2) * C)
+    take(yy(2) * C + 1)
+    lax.fori_loop(0, C, project, yy(2) * C)
     out_ref[...] = acc[...].astype(jnp.bfloat16)
 
     def sent(ref, sem):

time: 102 us -> 98.9 us (0.970)
  Pallas kernels: 99.9 us -> 95.9 us
    pallas_call x1, Pallas kernels: 99.9 us -> 95.9 us  [on_device(): pl.pallas_call(kernel, out_shape=jax.ShapeDtypeStruct((B * rows, rb), bf)...]
where the time goes in v3:
time: 98.9 us; the launch traced here: 97.6 us
  Pallas kernels  95.9 us (97%)
  local copies, waits for them, and re-layouts  1.67 us (2%)
    pallas_call x1, Pallas kernels, on_device(): pl.pallas_call(kernel, out_shape=jax.ShapeDtypeStruct((B * rows, rb), bf)...  95.9 us

profile of v3, /device:TPU:1, one launch (start us, length us, event | category | flops | bytes accessed | tf_op | source)
XLA Modules:
  0.0 97.6 jit_solution(16200792463330072495)
XLA Ops:
  0.0 95.9 %bjorck.1 = bf16[512,256]{1,0:T(8,128)(2,1)} custom-call(bf16[32,4096]{1,0:T(8,128)(2,1)} %t_ref.1, bf16[256,128]{1,0:T(8,128)(2,1)} %w_ref.1), custom_call_target="tpu_custom_call" | custom-call | tf_op jit(solution)/shard_map/bjorck/pallas_call | solution.py:426
  95.9 1.7 %copy.4 = bf16[512,256]{1,0:T(8,128)(2,1)} copy(bf16[512,256]{1,0:T(8,128)(2,1)} %bjorck.1) | data formatting | bytes 524288

commit v4 on v3

v4 whole, which is shorter than its diff:
```python
import functools

import jax
import jax.numpy as jnp
from jax import lax
from jax.experimental import pallas as pl
from jax.experimental.pallas import tpu as pltpu
from jax.sharding import PartitionSpec as P

MESH = pl.DeviceIdType.MESH
X, Y, H, L, C = 4, 4, 2, 8, 2
Z = H * L
B = X * H * C
LL = L // C
NC, FC = 2, 2


def dot_t(a, b):
    return lax.dot_general(a, b, (((1,), (1,)), ((), ())), preferred_element_type=jnp.float32)


def kernel(
    t_ref, w_ref, out_ref,
    zb, wc, rr, tb, pf, pr, ys, yr, gb, po, xb, xr, ob, oc, acc,
    loc, s_z, r_z, s_x, s_m, r_m, r_w, s_p, r_p, s_y, r_y, s_g, s_h, r_g, s_q, r_q,
    s_l, r_l, s_o, s_c, r_o, s_t, s_u, r_t,
):
    dp, tn = lax.axis_index("dp"), lax.axis_index("tensor")
    y, l = lax.div(dp, L), lax.rem(dp, L)
    x, h, c = lax.div(tn, H * C), lax.rem(lax.div(tn, C), H), lax.rem(tn, C)
    z = h * L + l
    other = 1 - c
    rb, cb = w_ref.shape
    rows = t_ref.shape[0]
    cw = LL * cb
    r = rb // LL
    zr, fr = rb // NC, r // FC

    def dev(ax, ay, az, ac):
        return (ay * L + lax.rem(az, L), (ax * H + lax.div(az, L)) * C + ac)

    def xs(k):
        return lax.rem(x + k, X)

    def yy(k):
        return lax.rem(y + k, Y)

    def zz(k):
        return lax.rem(z + k, Z)

    def send(src, dst, ssem, rsem, device):
        return pltpu.make_async_remote_copy(
            src_ref=src, dst_ref=dst, send_sem=ssem, recv_sem=rsem, device_id=device, device_id_type=MESH
        )

    def await_copy(ref, sem):
        pltpu.make_async_copy(ref, ref, sem).wait()

    def blk(ax, ah, ac):
        return (ax * H + ah) * C + ac

    def tblk(b):
        return tb.at[pl.ds(pl.multiple_of(b * rows, rows), rows), :]

    def part(ref, i):
        return ref.at[pl.ds(pl.multiple_of(i * r, r), r), :]

    mine, partner = blk(x, h, c), blk(x, 1 - h, c)
    loads = [pltpu.make_async_copy(w_ref.at[pl.ds(i * zr, zr), :], zb.at[z, i], loc.at[i]) for i in range(NC)]
    loads.append(pltpu.make_async_copy(t_ref, tblk(mine), loc.at[NC]))
    for load in loads:
        load.start()

    barrier = pltpu.get_barrier_semaphore()
    peers = [dev(x, y, zz(k), c) for k in (1, 2, 3, Z - 3, Z - 2, Z - 1)] + [dev(x, y, z, other)]
    peers += [dev(xs(k), y, z, a) for k in (1, 2, 3) for a in (c, other)]
    peers += [dev(x, yy(k), z, a) for k in (1, 2, 3) for a in (c, other)]
    for peer in peers:
        pl.semaphore_signal(barrier, inc=1, device_id=peer, device_id_type=MESH)
    pl.semaphore_wait(barrier, len(peers))
    for load in loads:
        load.wait()

    own_core, own_row = lax.div(l, LL), lax.rem(l, LL) * r
    own_chunk = lax.div(own_row, zr)

    def slot(b, i, k):
        return wc.at[b, pl.ds(i * zr, zr), pl.ds(pl.multiple_of(k * cb, cb), cb)]

    def go(q, i, k):
        send(zb.at[q, i], zb.at[q, i], s_z, r_z.at[q, i], dev(x, y, zz(k % Z), c)).start()

    def spread(q, i):
        lq, hq = lax.rem(q, L), lax.div(q, L)
        to, k = lax.div(lq, LL), lax.rem(lq, LL)
        b = hq * C + c

        @pl.when((hq == h) & (own_core == c) & (own_chunk == i))
        def _():
            src = zb.at[q, i, pl.ds(pl.multiple_of(own_row - i * zr, r), r), :]
            dst = rr.at[pl.ds(pl.multiple_of(x * r, r), r), pl.ds(pl.multiple_of(k * cb, cb), cb)]
            for n in (2, 1, 3):
                send(src, dst, s_m, r_m.at[x, k], dev(xs(n), y, z, to)).start()

        @pl.when(to != c)
        def _():
            send(zb.at[q, i], slot(b, i, k), s_x, r_w.at[b, i, k], dev(x, y, z, other)).start()

        @pl.when(to == c)
        def _():
            pltpu.make_async_copy(zb.at[q, i], slot(b, i, k), r_w.at[b, i, k]).start()

    def t_spread(b):
        for n in (2, 1, 3):
            send(tblk(b), tblk(b), s_u.at[n], r_t.at[b], dev(xs(n), y, z, c)).start()

    def t_other(b):
        send(tblk(b), tblk(b), s_u.at[0], r_t.at[b], dev(x, y, z, other)).start()

    def t_arrived(b):
        await_copy(tblk(b), r_t.at[b])
        t_other(b)
    for k in (3, 2, 1):
        for i in range(NC):
            go(z, i, k)
            go(z, i, -k)
    for i in range(NC):
        spread(z, i)
    t_spread(mine)
    t_other(mine)

    for n in range(1, Z // 2):
        for i in range(NC):
            for way in (1, -1):
                q = zz((-way * n) % Z)
                await_copy(zb.at[q, i], r_z.at[q, i])
                if n == 3:
                    for k in (3, 2, 1):
                        go(q, i, way * k)
                if n == 6:
                    if (way == 1) == (i < NC // 2):
                        go(q, i, way * 2)
                    go(q, i, way)
        for i in range(NC):
            for way in (1, -1):
                spread(zz((-way * n) % Z), i)
    q = zz(Z // 2)
    for i in range(NC):
        await_copy(zb.at[q, i], r_z.at[q, i])
        spread(q, i)
    send(tblk(mine), tblk(mine), s_t, r_t.at[mine], dev(x, y, zz(Z // 2), c)).start()
    for b in range(H * C):
        for i in range(NC):
            for k in range(LL):
                await_copy(slot(b, i, k), r_w.at[b, i, k])
    for n in (1, 2, 3):
        for k in range(LL):
            await_copy(
                rr.at[pl.ds(pl.multiple_of(xs(n) * r, r), r), pl.ds(k * cb, cb)], r_m.at[xs(n), k]
            )

    half = H * C // C
    wr = wc[h * C + own_core, pl.ds(pl.multiple_of(own_row, r), r), :]
    rr[pl.ds(pl.multiple_of(x * r, r), r), :] = wr
    for i in range(half):
        b = other * half + i
        pf[b] = dot_t(rr[...], wc[b])
    half_copy = send(pf.at[pl.ds(other * half, half)], pr, s_p, r_p, dev(x, y, z, other))
    half_copy.start()
    for i in range(half):
        b = c * half + i
        pf[b] = dot_t(rr[...], wc[b])
    half_copy.wait_recv()
    for i in range(half):
        total = pf[c * half + i] + pr[i]
        pf[c * half + i] = total
        ys[i] = total.astype(jnp.bfloat16)

    def y_part(ref, k):
        return ref.at[:, pl.ds(pl.multiple_of(k * r, r), r), :]

    for k in (2, 1, Y - 1):
        send(y_part(ys, yy(k)), yr.at[k], s_y.at[k], r_y.at[k], dev(x, yy(k), z, c)).start()
    for k in (1, Y - 1, 2):
        await_copy(yr.at[k], r_y.at[k])
    my_rows = pl.ds(pl.multiple_of(y * r, r), r)
    for n in (1, 3, 2):
        t_arrived(blk(xs(n), h, c))
    for i in range(half):
        total = pf[c * half + i, my_rows, :]
        for k in range(1, Y):
            total = total + yr[k, i].astype(jnp.float32)
        gb[c * half + i, my_rows, :] = total.astype(jnp.bfloat16)

    def g_at(a, k):
        return gb.at[pl.ds(a * half, half), pl.ds(pl.multiple_of(k * r, r), r), :]
    for k in (2, 1, Y - 1):
        send(g_at(c, y), g_at(c, y), s_g.at[k], r_g.at[c, y], dev(x, yy(k), z, c)).start()
    send(g_at(c, y), g_at(c, y), s_h.at[0], r_g.at[c, y], dev(x, y, z, other)).start()
    for k in (1, Y - 1, 2):
        await_copy(g_at(c, yy(k)), r_g.at[c, yy(k)])
        send(g_at(c, yy(k)), g_at(c, yy(k)), s_h.at[k], r_g.at[c, yy(k)], dev(x, y, z, other)).start()
    for k in range(Y):
        await_copy(g_at(other, yy(k)), r_g.at[other, yy(k)])

    total = jnp.dot(gb[0], wc[0], preferred_element_type=jnp.float32)
    for b in range(1, H * C):
        total = total + jnp.dot(gb[b], wc[b], preferred_element_type=jnp.float32)
    total = -0.5 * total
    po[...] = total
    xb[...] = total.astype(jnp.bfloat16)
    for n in (2, 1, 3):
        send(part(xb, xs(n)), xr.at[n], s_q.at[n], r_q.at[n], dev(xs(n), y, z, c)).start()
    for n in (1, 3, 2):
        await_copy(xr.at[n], r_q.at[n])
    total = 1.5 * wr.astype(jnp.float32) + po[pl.ds(pl.multiple_of(x * r, r), r), :]
    for n in (1, 2, 3):
        total = total + xr[n].astype(jnp.float32)
    for i in range(FC):
        ob[l, i] = total[i * fr:(i + 1) * fr].astype(jnp.bfloat16)

    def o_slot(a, k, i):
        return oc.at[a, pl.ds(pl.multiple_of(k * r + i * fr, fr), fr), :]

    def along(q, i, k, n):
        @pl.when((l + k >= 0) & (l + k < L))
        def _():
            send(ob.at[q, i], ob.at[q, i], s_l.at[n], r_l.at[q, i], (dp + k, tn)).start()

    def o_spread(q, i):
        to, k = lax.div(q, LL), lax.rem(q, LL)
        a = y * C + c
        dst, sem = o_slot(a, k, i), r_o.at[a, k, i]
        for n in (2, 1, 3):
            send(ob.at[q, i], dst, s_o.at[n], sem, dev(x, yy(n), z, to)).start()

        @pl.when(to != c)
        def _():
            send(ob.at[q, i], dst, s_c, sem, dev(x, y, z, other)).start()

        @pl.when(to == c)
        def _():
            pltpu.make_async_copy(ob.at[q, i], dst, sem).start()

    half_line = L // 2
    ways = [way * k for k in range(half_line, 0, -1) for way in (1, -1)]
    for i in range(FC):
        for n, k in enumerate(ways):
            along(l, i, k, n)
    for i in range(FC):
        o_spread(l, i)

    t_arrived(partner)
    t_spread(partner)
    for n in range(1, L):
        for i in range(FC):
            for way in (1, -1):
                q = l - way * n

                @pl.when((q >= 0) & (q < L))
                def _():
                    await_copy(ob.at[q, i], r_l.at[q, i])
                    if n == half_line:
                        for k in range(half_line - 1, 0, -1):
                            along(q, i, way * k, len(ways) + ways.index(way * k))
                    o_spread(q, i)
    for n in (1, 3, 2):
        t_arrived(blk(xs(n), 1 - h, c))
    for k in range(X):
        for hq in range(H):
            b = blk(xs(k), hq, other)
            await_copy(tblk(b), r_t.at[b])

    acc[...] = jnp.zeros_like(acc)

    def take(a):
        for k in range(LL):
            for i in range(FC):
                await_copy(o_slot(a, k, i), r_o.at[a, k, i])

    def project(i, first):
        a = lax.rem(first + i, Y * C)
        acc[...] += dot_t(tb[:, pl.ds(pl.multiple_of(a * cw, cw), cw)], oc[a])
        return first
    for k in (0, 1, Y - 1):
        take(yy(k) * C)
        take(yy(k) * C + 1)
    lax.fori_loop(0, 3 * C, project, yy(Y - 1) * C)
    take(yy(2) * C)
    take(yy(2) * C + 1)
    lax.fori_loop(0, C, project, yy(2) * C)
    out_ref[...] = acc[...].astype(jnp.bfloat16)

    def sent(ref, sem):
        pltpu.make_async_copy(ref, ref, sem).wait()
    sent(zb.at[pl.ds(0, Z - 1)], s_z)
    sent(zb.at[pl.ds(0, Z // 2)], s_x)

    @pl.when(own_core == c)
    def _():
        sent(zb.at[pl.ds(0, L * 3 // LL)], s_m)

    half_copy.wait_send()
    for k in range(1, Y):
        sent(yr.at[k], s_y.at[k])
        sent(yr.at[k], s_g.at[k])
        sent(xr.at[k], s_q.at[k])
    for k in range(Y):
        sent(yr.at[0], s_h.at[k])
    sent(tblk(mine), s_t)
    for n in (1, 2, 3):
        sent(tb.at[pl.ds(0, H * rows), :], s_u.at[n])
        sent(ob, s_o.at[n])
    sent(tb.at[pl.ds(0, X * H * rows), :], s_u.at[0])
    sent(ob.at[pl.ds(0, L // 2)], s_c)
    for n, k in enumerate(ways):
        @pl.when((l + k >= 0) & (l + k < L))
        def _():
            sent(ob.at[0], s_l.at[n])

        if abs(k) < half_line:
            far = l + k - (half_line if k > 0 else -half_line) - k

            @pl.when((l + k >= 0) & (l + k < L) & (far >= 0) & (far < L))
            def _():
                sent(ob.at[0], s_l.at[len(ways) + n])


def on_device(tokens, weight):
    rows, d = tokens.shape
    rb, cb = weight.shape
    cw, r, half = LL * cb, rb // LL, H
    dma = pltpu.SemaphoreType.DMA
    bf, f32 = jnp.bfloat16, jnp.float32
    return pl.pallas_call(
        kernel,
        out_shape=jax.ShapeDtypeStruct((B * rows, rb), bf),
        in_specs=[pl.BlockSpec(memory_space=pl.ANY)] * 2,
        out_specs=pl.BlockSpec(memory_space=pltpu.VMEM),
        scratch_shapes=[
            pltpu.VMEM((Z, NC, rb // NC, cb), bf),
            pltpu.VMEM((H * C, rb, cw), bf),
            pltpu.VMEM((X * r, cw), bf),
            pltpu.VMEM((B * rows, d), bf),
            pltpu.VMEM((H * C, X * r, rb), f32),
            pltpu.VMEM((half, X * r, rb), f32),
            pltpu.VMEM((half, X * r, rb), bf),
            pltpu.VMEM((Y, half, r, rb), bf),
            pltpu.VMEM((H * C, X * r, rb), bf),
            pltpu.VMEM((X * r, cw), f32),
            pltpu.VMEM((X * r, cw), bf),
            pltpu.VMEM((X, r, cw), bf),
            pltpu.VMEM((L, FC, r // FC, cw), bf),
            pltpu.VMEM((Y * C, rb, cw), bf),
            pltpu.VMEM((B * rows, rb), f32),
            dma((NC + 1,)),
            dma, dma((Z, NC)), dma, dma, dma((X, LL)), dma((H * C, NC, LL)),
            dma, dma, dma((Y,)), dma((Y,)), dma((Y,)), dma((Y,)), dma((C, Y)), dma((X,)), dma((X,)),
            dma((2 * L,)), dma((L, FC)), dma((Y,)), dma, dma((Y * C, LL, FC)),
            dma, dma((X,)), dma((B,)),
        ],
        compiler_params=pltpu.CompilerParams(
            collective_id=0, has_side_effects=True, vmem_limit_bytes=64_000_000
        ),
        name="bjorck",
    )(tokens, weight)


def solution(mesh):
    placed = (P(("dp", "tensor"), None), P("tensor", "dp"))
    return jax.shard_map(
        on_device, mesh=mesh, in_specs=placed, out_specs=P("dp", "tensor"), check_vma=False
    )
```

time: 98.9 us -> 101 us (1.021)
  Pallas kernels: 95.9 us -> 97.7 us
    pallas_call x1, Pallas kernels: 95.9 us -> 97.7 us  [on_device(): pl.pallas_call(kernel, out_shape=jax.ShapeDtypeStruct((B * rows, rb), bf)...]
where the time goes in v4:
time: 101 us; the launch traced here: 99.4 us
  Pallas kernels  97.7 us (97%)
  local copies, waits for them, and re-layouts  1.67 us (2%)
    pallas_call x1, Pallas kernels, on_device(): pl.pallas_call(kernel, out_shape=jax.ShapeDtypeStruct((B * rows, rb), bf)...  97.7 us

profile of v4, /device:TPU:1, one launch (start us, length us, event | category | flops | bytes accessed | tf_op | source)
XLA Modules:
  0.0 99.4 jit_solution(12502679464468233936)
XLA Ops:
  0.0 97.7 %bjorck.1 = bf16[512,256]{1,0:T(8,128)(2,1)} custom-call(bf16[32,4096]{1,0:T(8,128)(2,1)} %t_ref.1, bf16[256,128]{1,0:T(8,128)(2,1)} %w_ref.1), custom_call_target="tpu_custom_call" | custom-call | tf_op jit(solution)/shard_map/bjorck/pallas_call | solution.py:335
  97.7 1.7 %copy.4 = bf16[512,256]{1,0:T(8,128)(2,1)} copy(bf16[512,256]{1,0:T(8,128)(2,1)} %bjorck.1) | data formatting | bytes 524288

commit v5 on v3

--- a/solution.py
+++ b/solution.py
@@ -12,7 +12,7 @@
 Z = H * L
 B = X * H * C
 LL = L // C
-NC, FC = 4, 4
+NC, FC = 2, 4
 
 
 def dot_t(a, b):
@@ -75,9 +75,9 @@
         load.start()
 
     barrier = pltpu.get_barrier_semaphore()
-    peers = [dev(x, y, zz(1), c), dev(x, y, zz(Z - 1), c), dev(x, y, z, other)]
+    peers = [dev(x, y, zz(k), c) for k in (1, 2, Z - 2, Z - 1)] + [dev(x, y, z, other)]
     peers += [dev(xs(k), y, z, a) for k in (1, 2, 3) for a in (c, other)]
-    peers += [dev(x, yy(k), z, a) for k in (1, Y - 1) for a in (c, other)] + [dev(x, yy(2), z, c)]
+    peers += [dev(x, yy(k), z, a) for k in (1, 2, 3) for a in (c, other)]
     for peer in peers:
         pl.semaphore_signal(barrier, inc=1, device_id=peer, device_id_type=MESH)
     pl.semaphore_wait(barrier, len(peers))
@@ -90,11 +90,8 @@
     def slot(b, i, k):
         return wc.at[b, pl.ds(i * zr, zr), pl.ds(pl.multiple_of(k * cb, cb), cb)]
 
-    def up(q, i, sem=0):
-        send(zb.at[q, i], zb.at[q, i], s_z.at[sem], r_z.at[q, i], dev(x, y, zz(1), c)).start()
-
-    def down(q, i, sem=1):
-        send(zb.at[q, i], zb.at[q, i], s_z.at[sem], r_z.at[q, i], dev(x, y, zz(Z - 1), c)).start()
+    def go(q, i, k):
+        send(zb.at[q, i], zb.at[q, i], s_z, r_z.at[q, i], dev(x, y, zz(k % Z), c)).start()
 
     def spread(q, i):
         lq, hq = lax.rem(q, L), lax.div(q, L)
@@ -116,63 +113,43 @@
         def _():
             pltpu.make_async_copy(zb.at[q, i], slot(b, i, k), r_w.at[b, i, k]).start()
 
-    def t_spread(b):
-        send(tblk(b), tblk(b), s_u.at[0], r_t.at[b], dev(xs(1), y, z, c)).start()
-        send(tblk(b), tblk(b), s_u.at[1], r_t.at[b], dev(xs(X - 1), y, z, c)).start()
+    def t_spread(b, to):
+        for n in to:
+            send(tblk(b), tblk(b), s_u.at[n], r_t.at[b], dev(xs(n), y, z, c)).start()
 
     def t_other(b):
-        send(tblk(b), tblk(b), s_u.at[3], r_t.at[b], dev(x, y, z, other)).start()
-
-    def t_pass(hq, a, b):
-        near = blk(a, hq, c)
-        await_copy(tblk(near), r_t.at[near])
-        send(tblk(near), tblk(near), s_u.at[2], r_t.at[near], dev(b, y, z, c)).start()
-        t_other(near)
-
-    def t_turn(hq):
-        @pl.when(hq == 0)
-        def _():
-            t_pass(0, xs(X - 1), xs(1))
-
-        @pl.when(hq == 1)
-        def _():
-            t_pass(1, xs(1), xs(X - 1))
-    for i in range(NC):
-        up(z, i)
-        down(z, i)
+        send(tblk(b), tblk(b), s_u.at[0], r_t.at[b], dev(x, y, z, other)).start()
+
+    def t_arrived(b):
+        await_copy(tblk(b), r_t.at[b])
+        t_other(b)
+    for k in (2, 1):
+        for i in range(NC):
+            go(z, i, k)
+            go(z, i, -k)
     for i in range(NC):
         spread(z, i)
-    t_spread(mine)
+    t_spread(mine, (2, 1, 3))
     t_other(mine)
 
-    def z_step(s, _):
-        q, p = zz(Z - s), zz(s)
+    for n in range(1, Z // 2):
         for i in range(NC):
-            await_copy(zb.at[q, i], r_z.at[q, i])
-            up(q, i)
-            await_copy(zb.at[p, i], r_z.at[p, i])
-            down(p, i)
+            for way in (1, -1):
+                q = zz((-way * n) % Z)
+                await_copy(zb.at[q, i], r_z.at[q, i])
+                if n in (2, 4):
+                    for k in (2, 1):
+                        go(q, i, way * k)
+                if n == 6:
+                    if (way == 1) == (i < NC // 2):
+                        go(q, i, way * 2)
+                    go(q, i, way)
         for i in range(NC):
-            spread(q, i)
-            spread(p, i)
-        return 0
-    lax.fori_loop(1, Z // 2 - 1, z_step, 0)
-    q, p = zz(Z // 2 + 1), zz(Z // 2 - 1)
-    for i in range(NC):
-        await_copy(zb.at[q, i], r_z.at[q, i])
-        if i < NC // 2:
-            up(q, i, 2)
-        await_copy(zb.at[p, i], r_z.at[p, i])
-        if i >= NC // 2:
-            down(p, i, 3)
-    for i in range(NC):
-        spread(q, i)
-        spread(p, i)
-
+            for way in (1, -1):
+                spread(zz((-way * n) % Z), i)
     quarter = Z // 4
     send(thalf(mine, 0), t4.at[0], s_t.at[0], r_t4.at[0], dev(x, y, zz(quarter), c)).start()
     send(thalf(mine, 1), t4.at[1], s_t.at[1], r_t4.at[1], dev(x, y, zz(Z - quarter), c)).start()
-    t_turn(h)
     q = zz(Z // 2)
     for i in range(NC):
         await_copy(zb.at[q, i], r_z.at[q, i])
@@ -212,10 +189,8 @@
     for k in (1, Y - 1, 2):
         await_copy(yr.at[k], r_y.at[k])
     my_rows = pl.ds(pl.multiple_of(y * r, r), r)
-    for i, ahead, back in ((0, quarter, Z - quarter), (1, Z - quarter, quarter)):
-        await_copy(t4.at[i], r_t4.at[i])
-        home = blk(x, lax.div(zz(back), L), c)
-        send(t4.at[i], thalf(home, i), s_t.at[2 + i], r_tp.at[i], dev(x, y, zz(ahead), c)).start()
+    for n in (1, 3, 2):
+        t_arrived(blk(xs(n), h, c))
     for i in range(half):
         total = pf[c * half + i, my_rows, :]
         for k in range(1, Y):
@@ -230,6 +205,10 @@
     for k in (1, Y - 1, 2):
         await_copy(g_at(c, yy(k)), r_g.at[c, yy(k)])
         send(g_at(c, yy(k)), g_at(c, yy(k)), s_h.at[k], r_g.at[c, yy(k)], dev(x, y, z, other)).start()
+    for i, ahead, back in ((0, quarter, Z - quarter), (1, Z - quarter, quarter)):
+        await_copy(t4.at[i], r_t4.at[i])
+        home = blk(x, lax.div(zz(back), L), c)
+        send(t4.at[i], thalf(home, i), s_t.at[2 + i], r_tp.at[i], dev(x, y, zz(ahead), c)).start()
     for k in range(Y):
         await_copy(g_at(other, yy(k)), r_g.at[other, yy(k)])
 
@@ -324,16 +303,20 @@
         def _():
             o_relay(l + s - 2)
 
-        @pl.when(s == 1)
+        @pl.when(s == 2)
         def _():
             await_copy(thalf(partner, 0), r_tp.at[0])
             await_copy(thalf(partner, 1), r_tp.at[1])
-            t_spread(partner)
+            t_spread(partner, (1, 3))
             t_other(partner)
 
-        @pl.when(s == 4)
-        def _():
-            t_turn(1 - h)
+        @pl.when(s == 5)
+        def _():
+            for i, near, far in ((0, xs(3), xs(1)), (1, xs(1), xs(3))):
+                b = blk(near, 1 - h, c)
+                await_copy(tblk(b), r_t.at[b])
+                send(thalf(b, i), thalf(b, i), s_u.at[X + i], r_t.at[b], dev(far, y, z, c)).start()
+                t_other(b)
 
         return 0
     lax.fori_loop(1, L, l_step, 0)
@@ -345,10 +328,7 @@
         @pl.when(l + s < L)
         def _():
             o_relay(l + s)
-    for hq, a in ((1, xs(X - 1)), (0, xs(1)), (0, xs(2)), (1, xs(2))):
-        b = blk(a, hq, c)
-        await_copy(tblk(b), r_t.at[b])
-        t_other(b)
+    t_arrived(blk(xs(2), 1 - h, c))
     for k in range(X):
         for hq in range(H):
             b = blk(xs(k), hq, other)
@@ -375,9 +355,7 @@
 
     def sent(ref, sem):
         pltpu.make_async_copy(ref, ref, sem).wait()
-    for n in range(2):
-        sent(zb.at[pl.ds(0, Z // 2 - 1)], s_z.at[n])
-        sent(zb.at[0, pl.ds(0, NC // 2)], s_z.at[2 + n])
+    sent(zb.at[pl.ds(0, Z - 1)], s_z)
     sent(zb.at[pl.ds(0, Z // 2)], s_x)
 
     @pl.when(own_core == c)
@@ -393,16 +371,16 @@
         sent(yr.at[0], s_h.at[k])
     for k in range(4):
         sent(t4.at[0], s_t.at[k])
-    two, eight = tb.at[pl.ds(0, H * rows), :], tb.at[pl.ds(0, X * H * rows), :]
-    sent(two, s_u.at[0])
-    sent(two, s_u.at[1])
-    sent(two, s_u.at[2])
-    sent(eight, s_u.at[3])
+    sent(tb.at[pl.ds(0, H * rows), :], s_u.at[1])
+    sent(tblk(mine), s_u.at[2])
+    sent(tb.at[pl.ds(0, H * rows), :], s_u.at[3])
+    sent(thalf(mine, 0), s_u.at[X])
+    sent(thalf(mine, 1), s_u.at[X + 1])
+    sent(tb.at[pl.ds(0, X * H * rows), :], s_u.at[0])
     sent(ob, s_o.at[0])
     sent(ob, s_o.at[1])
     sent(ob.at[pl.ds(0, L // 2)], s_c)
     sent(ob, s_r)
-
     def line(q, _):
         @pl.when((l < L - 1) & (q <= l))
         def _():
@@ -446,10 +424,10 @@
             pltpu.VMEM((Y * C, rb, cw), bf),
             pltpu.VMEM((B * rows, rb), f32),
             dma((NC + 1,)),
-            dma((4,)), dma((Z, NC)), dma, dma, dma((X, LL)), dma((H * C, NC, LL)),
+            dma, dma((Z, NC)), dma, dma, dma((X, LL)), dma((H * C, NC, LL)),
             dma, dma, dma((Y,)), dma((Y,)), dma((Y,)), dma((Y,)), dma((C, Y)), dma((X,)), dma((X,)),
             dma((2, L)), dma((L, FC)), dma((2,)), dma, dma, dma((Y * C, LL, FC)),
-            dma((4,)), dma((2,)), dma((2,)), dma((4,)), dma((B,)),
+            dma((4,)), dma((2,)), dma((2,)), dma((X + 2,)), dma((B,)),
         ],
         compiler_params=pltpu.CompilerParams(
             collective_id=0, has_side_effects=True, vmem_limit_bytes=64_000_000

time: 98.9 us -> 95 us (0.961); the launches traced: 97.6 us -> 94.8 us
  Pallas kernels: 95.9 us -> 93.2 us
    pallas_call x1, Pallas kernels: 95.9 us -> 93.2 us  [on_device(): pl.pallas_call(kernel, out_shape=jax.ShapeDtypeStruct((B * rows, rb), bf)...]
where the time goes in v5:
time: 95 us; the launch traced here: 94.8 us
  Pallas kernels  93.2 us (98%)
  local copies, waits for them, and re-layouts  1.67 us (2%)
    pallas_call x1, Pallas kernels, on_device(): pl.pallas_call(kernel, out_shape=jax.ShapeDtypeStruct((B * rows, rb), bf)...  93.2 us

profile of v5, /device:TPU:1, one launch (start us, length us, event | category | flops | bytes accessed | tf_op | source)
XLA Modules:
  0.0 94.8 jit_solution(15031955083970913152)
XLA Ops:
  0.0 93.2 %bjorck.1 = bf16[512,256]{1,0:T(8,128)(2,1)} custom-call(bf16[32,4096]{1,0:T(8,128)(2,1)} %t_ref.1, bf16[256,128]{1,0:T(8,128)(2,1)} %w_ref.1), custom_call_target="tpu_custom_call" | custom-call | tf_op jit(solution)/shard_map/bjorck/pallas_call | solution.py:404
  93.2 1.7 %copy.4 = bf16[512,256]{1,0:T(8,128)(2,1)} copy(bf16[512,256]{1,0:T(8,128)(2,1)} %bjorck.1) | data formatting | bytes 524288

commit v6 on v5

--- a/solution.py
+++ b/solution.py
@@ -144,9 +144,7 @@
                     if (way == 1) == (i < NC // 2):
                         go(q, i, way * 2)
                     go(q, i, way)
-        for i in range(NC):
-            for way in (1, -1):
-                spread(zz((-way * n) % Z), i)
+                spread(q, i)
     quarter = Z // 4
     send(thalf(mine, 0), t4.at[0], s_t.at[0], r_t4.at[0], dev(x, y, zz(quarter), c)).start()
     send(thalf(mine, 1), t4.at[1], s_t.at[1], r_t4.at[1], dev(x, y, zz(Z - quarter), c)).start()
@@ -276,19 +274,12 @@
             def _():
                 await_copy(ob.at[l - s, i], r_l.at[l - s, i])
                 o_up(l - s, i)
+                o_spread(l - s, i)
 
             @pl.when(l + s < L)
             def _():
                 await_copy(ob.at[l + s, i], r_l.at[l + s, i])
                 o_down(l + s, i)
-
-        for i in range(FC):
-            @pl.when(l - s >= 0)
-            def _():
-                o_spread(l - s, i)
-
-            @pl.when(l + s < L)
-            def _():
                 o_spread(l + s, i)
 
         @pl.when(s == 2)

time: 95 us -> 95 us (level)
  no operation moved by 1% of the time
where the time goes in v6:
time: 95 us; the launch traced here: 94.8 us
  Pallas kernels  93.1 us (98%)
  local copies, waits for them, and re-layouts  1.67 us (2%)
    pallas_call x1, Pallas kernels, on_device(): pl.pallas_call(kernel, out_shape=jax.ShapeDtypeStruct((B * rows, rb), bf)...  93.1 us

profile of v6, /device:TPU:1, one launch (start us, length us, event | category | flops | bytes accessed | tf_op | source)
XLA Modules:
  0.0 94.8 jit_solution(16851074973136622258)
XLA Ops:
  0.0 93.1 %bjorck.1 = bf16[512,256]{1,0:T(8,128)(2,1)} custom-call(bf16[32,4096]{1,0:T(8,128)(2,1)} %t_ref.1, bf16[256,128]{1,0:T(8,128)(2,1)} %w_ref.1), custom_call_target="tpu_custom_call" | custom-call | tf_op jit(solution)/shard_map/bjorck/pallas_call | solution.py:395
  93.1 1.7 %copy.4 = bf16[512,256]{1,0:T(8,128)(2,1)} copy(bf16[512,256]{1,0:T(8,128)(2,1)} %bjorck.1) | data formatting | bytes 524288
